TPU v7x, 512 devices: a whole 4x8x8 slice. The times are simulated.
512 devices in a mesh: outer: 16 (over y, core), inner: 32 (over x, z).
Axes of the slice: x: 4, y: 8, z: 8, core: 2. Of those that a mesh axis runs over, the one named last changes fastest.
Arguments:
- queries: bfloat16 [32768, 4096], P('inner', 'outer'), may hold values from -150 to 150
- keys: bfloat16 [32768, 4096], P('inner', 'outer'), may hold values from -7 to 7
- values: bfloat16 [32768, 4096], P('inner', 'outer'), may hold values from -18 to 18
- counts: int32 [256], P('inner'), may hold values from 1 to 128, 24576 in all
- window_mask: int32 [256, 3], P('inner'), may hold values 0 or 1
- norm_gain: float32 [4096], P('outer'), may hold values from 0.5 to 1.5
Outputs:
- attended: bfloat16 [32768, 4096], P('inner', 'outer')
Inputs may be any that keep to these rules, and one draw needn't show every extreme that they name: `counts`: the largest count is exactly 128.
All inputs are finite; a program needn't handle non-finite values. No bound on the sum of `counts` or of `window_mask` on one device may be relied on, other than what follows from the above.
Results may differ from a plain program's by a relative error of at most 0.0048.
Values may be sent and summed in bfloat16 or wider, within the bound.
A program may use at most 64 MiB of HBM per device.

v0:
```python
import jax
import jax.numpy as jnp
from jax import lax
from jax.sharding import PartitionSpec as P

HD = 128
BLK = 128
PREV = 3
WIDTH = 4096


def carried_in(part, axis, combine, identity):
    place = lax.axis_index(axis)
    gathered = lax.all_gather(part, axis)
    state = jnp.zeros_like(part) + jnp.asarray(identity, part.dtype)

    def one(step, state):
        return combine(state, lax.dynamic_index_in_dim(gathered, step, 0, False))

    return lax.fori_loop(0, place, one, state)


def from_behind(value, axis, steps):
    count = lax.axis_size(axis)
    first, last = (max(0, -steps), min(count, count - steps))
    return lax.ppermute(value, axis, [(source, source + steps) for source in range(first, last)])


def add_states(earlier, later):
    return earlier + later


def shards(queries, keys, values, counts, window_mask, norm_gain):
    tok_rows = queries.shape[0]
    groups_here = tok_rows // BLK
    local_heads = queries.shape[1] // HD
    position = lax.broadcasted_iota(jnp.int32, (BLK,), 0)
    key_valid = position[None, :] < counts[:, None]
    masked_keys = jnp.where(key_valid.reshape(tok_rows)[:, None], keys, jnp.zeros((), jnp.bfloat16))
    query_blocks = queries.reshape(groups_here, BLK, local_heads, HD)
    key_blocks = masked_keys.reshape(groups_here, BLK, local_heads, HD)
    value_blocks = values.reshape(groups_here, BLK, local_heads, HD)
    group_states = jnp.einsum(
        "cshd,cshe->chde", key_blocks, value_blocks, preferred_element_type=jnp.float32
    )
    running = jnp.cumsum(group_states, axis=0)
    within = jnp.concatenate([jnp.zeros_like(group_states[:1]), running[:-1]], axis=0)
    span_total = running[-1]
    before = carried_in(span_total, "inner", add_states, jnp.zeros_like(span_total))
    prior_rounded = (before[None] + within).astype(jnp.bfloat16)
    rim_rows = PREV * BLK
    rim_keys, rim_values, rim_counts = from_behind(
        (
            masked_keys[tok_rows - rim_rows :],
            values[tok_rows - rim_rows :],
            counts[groups_here - PREV :],
        ),
        "inner",
        1,
    )
    extended_keys = jnp.concatenate([rim_keys, masked_keys], axis=0).reshape(
        groups_here + PREV, BLK, local_heads, HD
    )
    extended_values = jnp.concatenate([rim_values, values], axis=0).reshape(
        groups_here + PREV, BLK, local_heads, HD
    )
    extended_counts = jnp.concatenate([rim_counts, counts], axis=0)
    extended_valid = position[None, :] < extended_counts[:, None]
    window_keys = jnp.stack(
        [extended_keys[place : place + groups_here] for place in range(PREV + 1)], axis=1
    ).reshape(groups_here, (PREV + 1) * BLK, local_heads, HD)
    window_values = jnp.stack(
        [extended_values[place : place + groups_here] for place in range(PREV + 1)], axis=1
    ).reshape(groups_here, (PREV + 1) * BLK, local_heads, HD)
    window_valid = jnp.stack(
        [extended_valid[place : place + groups_here] for place in range(PREV + 1)], axis=1
    )
    group_on = jnp.concatenate(
        [window_mask[:, ::-1] == 1, jnp.ones((groups_here, 1), jnp.bool_)], axis=1
    )
    causal = position[:, None] >= position[None, :]
    causal_full = jnp.concatenate([jnp.ones((BLK, PREV * BLK), jnp.bool_), causal], axis=1)
    allowed = (window_valid & group_on[:, :, None]).reshape(
        groups_here, 1, (PREV + 1) * BLK
    ) & causal_full[None]
    score_scale = 1.0 / HD**0.5
    scores = (
        jnp.einsum("cthd,cshd->chts", query_blocks, window_keys, preferred_element_type=jnp.float32)
        * score_scale
    )
    scores = jnp.where(allowed[:, None], scores, -1e30)
    largest = jnp.max(scores, axis=-1, keepdims=True)
    expd = jnp.exp(scores - largest)
    weights = (expd / jnp.sum(expd, axis=-1, keepdims=True)).astype(jnp.bfloat16)
    local_part = jnp.einsum(
        "chts,cshd->cthd", weights, window_values, preferred_element_type=jnp.float32
    )
    inter = jnp.einsum(
        "cthd,chde->cthe", query_blocks, prior_rounded, preferred_element_type=jnp.float32
    )
    intra_weights = jnp.einsum(
        "cthd,cshd->chts", query_blocks, key_blocks, preferred_element_type=jnp.float32
    )
    intra_weights = jnp.where(causal[None, None], intra_weights, 0.0).astype(jnp.bfloat16)
    intra = jnp.einsum(
        "chts,cshe->cthe", intra_weights, value_blocks, preferred_element_type=jnp.float32
    )
    linear_part = inter + intra
    local_squares = jnp.sum(linear_part * linear_part, axis=(2, 3))
    row_squares = lax.psum(local_squares, "outer")
    normed = linear_part * lax.rsqrt(row_squares / WIDTH + 1e-06)[:, :, None, None]
    result = normed * norm_gain.reshape(local_heads, HD)[None, None] + local_part
    return result.reshape(tok_rows, local_heads * HD).astype(jnp.bfloat16)


def solution(mesh):
    return jax.shard_map(
        shards,
        mesh=mesh,
        in_specs=(
            P("inner", "outer"),
            P("inner", "outer"),
            P("inner", "outer"),
            P("inner"),
            P("inner", None),
            P("outer"),
        ),
        out_specs=P("inner", "outer"),
        check_vma=False,
    )
```

profile of v0, /device:TPU:7, one launch (start us, length us, event | category | flops | bytes accessed | tf_op | source)
XLA Modules:
  0.0 166.0 jit_solution(16054141134522092386)
XLA Ops:
  7.3 1.2 broadcast_select_fusion
  8.7 1.2 reshape.85
  10.8 1.1 fusion.38
  13.4 4.0 %collective-permute-start.2 = (bf16[384,256]{1,0:T(8,128)(2,1)}, bf16[384,256]{1,0:T(8,128)(2,1)S(1)}, u32[]{:S(2)}, u32[]{:S(2)}) collective-permute-start(bf16[384,256]{1,0:T(8,128)(2,1)} %slice.79), channel_id=1, source_target_pairs={{0,1},{1,2},{2,3},{3,4},{4,5},{5,6},{6,7},{7,8},{8,9},{9,10},{10,1... | collective-permute-start | bytes 589832 | tf_op jit(solution)/shard_map/ppermute | solution.py:26
  18.1 4.0 %collective-permute-start.1 = (s32[3]{0:T(128)}, s32[3]{0:T(128)}, u32[]{:S(2)}, u32[]{:S(2)}) collective-permute-start(s32[3]{0:T(128)} %slice.61), channel_id=1, source_target_pairs={{0,1},{1,2},{2,3},{3,4},{4,5},{5,6},{6,7},{7,8},{8,9},{9,10},{10,1... | collective-permute-start | bytes 44 | tf_op jit(solution)/shard_map/ppermute | solution.py:26
  22.8 4.0 %collective-permute-start = (bf16[384,256]{1,0:T(8,128)(2,1)}, bf16[384,256]{1,0:T(8,128)(2,1)S(1)}, u32[]{:S(2)}, u32[]{:S(2)}) collective-permute-start(bf16[384,256]{1,0:T(8,128)(2,1)} %slice.57), channel_id=1, source_target_pairs={{0,1},{1,2},{2,3},{3,4},{4,5},{5,6},{6,7},{7,8},{8,9},{9,10},{10,1... | collective-permute-start | bytes 589832 | tf_op jit(solution)/shard_map/ppermute | solution.py:26
  28.6 2.0 %copy.56 = bf16[8,1,128,2,128]{4,2,1,3,0:T(8,128)(2,1)} copy(bf16[8,1,128,2,128]{4,3,2,0,1:T(2,128)(2,1)} %stack.58) | data formatting | bytes 1048576 | tf_op jit(solution)/shard_map/stack | solution.py:69
  30.6 1.2 reshape.86
  31.9 3.8 %copy.52 = bf16[8,1,128,2,128]{2,1,4,3,0:T(2,128)(2,1)} copy(bf16[8,1,128,2,128]{4,3,2,0,1:T(2,128)(2,1)} %stack.48) | data formatting | bytes 1048576 | tf_op jit(solution)/shard_map/stack | solution.py:72
  36.6 1.4 broadcast_and_fusion
  38.9 1.2 stack.55
  43.1 1.1 fusion.32
  44.2 1.2 stack.45
  45.4 2.0 %copy.49 = bf16[8,1,128,2,128]{2,1,4,3,0:T(2,128)(2,1)} copy(bf16[8,1,128,2,128]{4,3,2,0,1:T(2,128)(2,1)S(1)} %stack.45) | data formatting | bytes 1048576 | tf_op jit(solution)/shard_map/stack | solution.py:72
  47.4 1.2 stack.46
  48.6 2.0 %copy.50 = bf16[8,1,128,2,128]{2,1,4,3,0:T(2,128)(2,1)} copy(bf16[8,1,128,2,128]{4,3,2,0,1:T(2,128)(2,1)S(1)} %stack.46) | data formatting | bytes 1048576 | tf_op jit(solution)/shard_map/stack | solution.py:72
  50.7 2.0 %copy.51 = bf16[8,1,128,2,128]{2,1,4,3,0:T(2,128)(2,1)} copy(bf16[8,1,128,2,128]{4,3,2,0,1:T(2,128)(2,1)S(1)} %stack.47) | data formatting | bytes 1048576 | tf_op jit(solution)/shard_map/stack | solution.py:72
  52.7 6.4 %pad_maximum_fusion = bf16[8,4,128,2,128]{2,1,4,3,0:T(4,128)(2,1)S(1)} fusion(bf16[8,1,128,2,128]{2,1,4,3,0:T(2,128)(2,1)} %copy.52, bf16[8,1,128,2,128]{2,1,4,3,0:T(2,128)(2,1)} %copy.51, bf16[8,1,128,2,128]{2,1,4,3,0:T(2,128)(2,1)} %copy.50, bf16[8,1,128,2,128]{2,1,4,3,0:T(2,128)(2,1)} %copy.49), kind=kLoop, calls=%fused_computation.6 | loop fusion | flops 8388608 | bytes 4194304 | tf_op jit(solution)/shard_map/stack | solution.py:72
  59.1 2.2 %reshape.87 = bf16[8,512,2,128]{1,3,2,0:T(8,128)(2,1)} reshape(bf16[8,4,128,2,128]{2,1,4,3,0:T(4,128)(2,1)S(1)} %pad_maximum_fusion) | data formatting | bytes 4194304 | tf_op jit(solution)/shard_map/reshape | solution.py:74
  61.3 1.8 %pad_maximum_fusion.1 = bf16[8,4,128,2,128]{4,2,1,3,0:T(8,128)(2,1)S(1)} fusion(bf16[8,1,128,2,128]{4,2,1,3,0:T(8,128)(2,1)} %copy.56, bf16[8,1,128,2,128]{4,2,1,3,0:T(8,128)(2,1)} %copy.55, bf16[8,1,128,2,128]{4,2,1,3,0:T(8,128)(2,1)} %copy.54, bf16[8,1,128,2,128]{4,2,1,3,0:T(8,128)(2,1)} %copy.53), kind=kLoop, calls=%fused_computation.7 | loop fusion | flops 3145728 | bytes 4194304 | tf_op jit(solution)/shard_map/stack | solution.py:69
  64.2 3.9 %fusion.33 = (f32[8,2,128]{2,1,0:T(2,128)S(1)}, f32[8,2,128,512]{2,3,1,0:T(8,128)}) fusion(f32[8,2,512,128]{3,2,1,0:T(8,128)S(1)} %fusion.21, pred[8,128,512]{1,2,0:T(8,128)(4,1)S(1)} %copy-done.4), kind=kOutput, calls=%fused_computation.63 | output fusion | flops 6291967 | bytes 8921088 | tf_op jit(solution)/shard_map/sub | solution.py:93
  68.0 32.9 %all-gather.2.cloned.1.call-done = f32[32,2,128,128]{3,2,1,0:T(8,128)} async-done(((f32[1,2,128,128]{3,2,1,0:T(8,128)}), f32[32,2,128,128]{3,2,1,0:T(8,128)}) %all-gather.2.cloned.1.call-update) | async-done | bytes 4194320 | tf_op jit(solution)/shard_map/all_gather | solution.py:14
  100.9 23.1 %while.10 = (s32[]{:T(128)}, f32[2,128,128]{2,1,0:T(8,128)S(1)}, s32[]{:T(128)}, f32[32,2,128,128]{3,2,1,0:T(8,128)}, s32[]{:T(128)}, /*index=5*/s32[]{:T(128)}, s32[]{:T(128)}) while((s32[]{:T(128)}, f32[2,128,128]{2,1,0:T(8,128)S(1)}, s32[]{:T(128)}, f32[32,2,128,128]{3,2,1,0:T(8,128)}, s32[]{:T(128)}, /*index=5*/s32[]{:T(128)}, ...), condition=%wide.region_2.3_spmd, body=%wide.region_1.2_spmd.sunk | while | flops 32773 | bytes 393331 | solution.py:20
  101.0 0.9 bitcast_add_fusion.2
  101.9 0.9 bitcast_add_fusion.2
  102.9 0.9 bitcast_add_fusion.2
  107.7 0.9 bitcast_add_fusion.2
  109.7 0.9 bitcast_add_fusion.2
  124.1 1.5 convolution_bitcast_fusion.2
  125.6 1.9 %multiply_reduce_fusion = (f32[8,128]{1,0:T(8,128)S(1)}, f32[8,128,2,128]{1,3,2,0:T(8,128)S(1)}) fusion(f32[8,128,2,128]{1,3,2,0:T(8,128)} %convolution_bitcast_fusion.2, bf16[8,128,2,128]{1,3,2,0:T(8,128)(2,1)S(1)} %copy-done.2, pred[128,128]{0,1:T(8,128)(4,1)S(1)} %iota_compare_fusion, bf16[8,128,2,128]{3,2,1,0:T(2,128)(2,1)S(1)} %reshape.84, ...), kind=kOutput, calls=%fused_computation.21 | convolution fusion | flops 135527424 | bytes 3690496 | tf_op jit(solution)/shard_map/chts,cshe->cthe/dot_general | solution.py:105
  127.5 26.7 %psum.7 = f32[8,128]{1,0:T(8,128)S(1)} all-reduce(f32[8,128]{1,0:T(8,128)S(1)} %get-tuple-element.49), channel_id=1, replica_groups=mesh['outer'=16,'inner'=32] {'outer'}, use_global_device_ids=true, to_apply=%region_4.5 | all-reduce | flops 1024 | bytes 8192 | tf_op jit(solution)/shard_map/psum | solution.py:110
  154.2 3.5 %fusion.10 = bf16[8,128,2,128]{1,3,2,0:T(8,128)(2,1)S(1)} fusion(bf16[8,512,2,128]{1,3,2,0:T(8,128)(2,1)} %reshape.87, f32[8,2,128,512]{2,3,1,0:T(8,128)} %get-tuple-element.48, f32[8,2,128]{2,1,0:T(2,128)S(1)} %get-tuple-element.47, f32[8,128,2,128]{1,3,2,0:T(8,128)S(1)} %get-tuple-element.50, f32[2,128]{1,0:T(2,128)S(1)} %bitcast.65, ...), kind=kOutput, calls=%fused_computation.19 | convolution fusion | flops 271581184 | bytes 7877632 | tf_op jit(solution)/shard_map/chts,cshd->cthd/dot_general | solution.py:95
  (75 shorter events, 31.7 us)
Async XLA Ops:
  6.5 94.4 %all-gather.2.cloned.1.call-start = ((), (), s32[]{:S(2)}) async-start(), calls=%async_computation | async-start | bytes 4325376 | tf_op jit(solution)/shard_map/all_gather | solution.py:14
  8.5 8.9 %copy-start.7 = (s32[8]{0:T(128)S(1)}, s32[8]{0:T(128)}, u32[]{:S(2)}) copy-start(s32[8]{0:T(128)} %param.11) | copy-start | bytes 100
  8.5 13.5 %copy-start = (bf16[1024,256]{1,0:T(8,128)(2,1)S(1)}, bf16[1024,256]{1,0:T(8,128)(2,1)}, u32[]{:S(2)}) copy-start(bf16[1024,256]{1,0:T(8,128)(2,1)} %param.10) | copy-start | bytes 1572868
  10.3 18.3 %copy-start.1 = (bf16[8,128,2,128]{1,3,2,0:T(8,128)(2,1)}, bf16[8,128,2,128]{1,3,2,0:T(8,128)(2,1)S(1)}, u32[]{:S(2)}) copy-start(bf16[8,128,2,128]{1,3,2,0:T(8,128)(2,1)S(1)} %copy.48) | copy-start | bytes 1572868
  10.8 20.9 %copy-start.5 = (s32[8,3]{0,1:T(4,128)S(1)}, s32[8,3]{0,1:T(4,128)}, u32[]{:S(2)}) copy-start(s32[8,3]{0,1:T(4,128)} %param.12) | copy-start | bytes 292
  11.9 16.6 %copy-start.3 = (f32[8,2,128,128]{3,2,1,0:T(8,128)}, f32[8,2,128,128]{3,2,1,0:T(8,128)S(1)}, u32[]{:S(2)}) copy-start(f32[8,2,128,128]{3,2,1,0:T(8,128)S(1)} %fusion.38) | copy-start | bytes 3145732
  13.4 24.6 %collective-permute-start.2 = (bf16[384,256]{1,0:T(8,128)(2,1)}, bf16[384,256]{1,0:T(8,128)(2,1)S(1)}, u32[]{:S(2)}, u32[]{:S(2)}) collective-permute-start(bf16[384,256]{1,0:T(8,128)(2,1)} %slice.79), channel_id=1, source_target_pairs={{0,1},{1,2},{2,3},{3,4},{4,5},{5,6},{6,7},{7,8},{8,9},{9,10},{10,1... | collective-permute-start | bytes 589832 | tf_op jit(solution)/shard_map/ppermute | solution.py:26
  18.1 17.6 %collective-permute-start.1 = (s32[3]{0:T(128)}, s32[3]{0:T(128)}, u32[]{:S(2)}, u32[]{:S(2)}) collective-permute-start(s32[3]{0:T(128)} %slice.61), channel_id=1, source_target_pairs={{0,1},{1,2},{2,3},{3,4},{4,5},{5,6},{6,7},{7,8},{8,9},{9,10},{10,1... | collective-permute-start | bytes 44 | tf_op jit(solution)/shard_map/ppermute | solution.py:26
  22.8 20.3 %collective-permute-start = (bf16[384,256]{1,0:T(8,128)(2,1)}, bf16[384,256]{1,0:T(8,128)(2,1)S(1)}, u32[]{:S(2)}, u32[]{:S(2)}) collective-permute-start(bf16[384,256]{1,0:T(8,128)(2,1)} %slice.57), channel_id=1, source_target_pairs={{0,1},{1,2},{2,3},{3,4},{4,5},{5,6},{6,7},{7,8},{8,9},{9,10},{10,1... | collective-permute-start | bytes 589832 | tf_op jit(solution)/shard_map/ppermute | solution.py:26
  63.1 1.0 copy-start.4
  64.2 59.9 %slice-start = ((f32[8,2,128,128]{3,2,1,0:T(8,128)}), f32[7,2,128,128]{3,2,1,0:T(8,128)S(1)}, s32[]{:S(2)}) async-start(f32[8,2,128,128]{3,2,1,0:T(8,128)} %copy-done.3), calls=%async_computation.1 | async-start | bytes 1835008 | tf_op jit(solution)/shard_map/slice | solution.py:47
  68.0 57.6 %copy-start.2 = (bf16[8,128,2,128]{1,3,2,0:T(8,128)(2,1)S(1)}, bf16[8,128,2,128]{1,3,2,0:T(8,128)(2,1)}, u32[]{:S(2)}) copy-start(bf16[8,128,2,128]{1,3,2,0:T(8,128)(2,1)} %copy-done.1) | copy-start | bytes 1572868
  100.9 53.3 %copy-start.6 = (f32[256]{0:T(256)S(1)}, f32[256]{0:T(256)}, u32[]{:S(2)}) copy-start(f32[256]{0:T(256)} %param.13) | copy-start | bytes 3076
Sparse Core Ops, SparseCore 0:
  12.8 88.0 all-gather.1
where the time goes:
time: 167 us; the launch traced here: 166 us
  other arithmetic  40.8 us (24%)
  waiting for transfers between devices  32.9 us (20%)
  local copies, waits for them, and re-layouts  31 us (19%)
  blocking collectives  26.7 us (16%)
  between operations  13.6 us (8%)
  starting transfers between devices  12 us (7%)
  matrix products  8.16 us (5%)
    all_gather x1, waiting for transfers between devices, carried_in(): gathered = lax.all_gather(part, axis)  32.9 us
    psum x1, blocking collectives, shards(): row_squares = lax.psum(local_squares, 'outer')  26.7 us
    add x24, other arithmetic, add_states(): return earlier + later  22.5 us
    another operation x8, local copies, waits for them, and re-layouts, shards(): jnp.stack([extended_values[place:place + groups_here] for place in range(...  13.2 us
    ppermute x3, starting transfers between devices, from_behind(): lax.ppermute(value, axis, [(source, source + steps) for source in range(f...  12 us
    another operation x8, local copies, waits for them, and re-layouts, shards(): jnp.stack([extended_keys[place:place + groups_here] for place in range(PR...  7.08 us
    another operation x1, other arithmetic, shards(): jnp.stack([extended_values[place:place + groups_here] for place in range(...  6.43 us
    sub x1, other arithmetic, shards(): expd = jnp.exp(scores - largest)  3.88 us
  transfers between devices with their start and end apart: 4, of which 1 were waited for; matrix products, arithmetic and copies ran while one was open for 26% of the time, Pallas kernels for 0%

commit v1 on v0

--- a/solution.py
+++ b/solution.py
@@ -107,7 +107,11 @@
     )
     linear_part = inter + intra
     local_squares = jnp.sum(linear_part * linear_part, axis=(2, 3))
-    row_squares = lax.psum(local_squares, "outer")
+    row_squares = local_squares
+    for hop in (1, 2, 4, 8):
+        row_squares = row_squares + lax.ppermute(
+            row_squares, "outer", [(dev, dev ^ hop) for dev in range(16)]
+        )
     normed = linear_part * lax.rsqrt(row_squares / WIDTH + 1e-06)[:, :, None, None]
     result = normed * norm_gain.reshape(local_heads, HD)[None, None] + local_part
     return result.reshape(tok_rows, local_heads * HD).astype(jnp.bfloat16)

time: 167 us -> 181 us (1.084)
  blocking collectives: 26.7 us -> 0 us
  waiting for transfers between devices: 32.9 us -> 53.8 us
  starting transfers between devices: 12 us -> 30.4 us
  matrix products: 8.16 us -> 10.6 us
  local copies, waits for them, and re-layouts: 31 us -> 29 us
    psum x1 -> x0, blocking collectives: 26.7 us -> none  [shards(): row_squares = lax.psum(local_squares, 'outer')]
    all_gather x1, waiting for transfers between devices: 32.9 us -> 52.6 us  [carried_in(): gathered = lax.all_gather(part, axis)]
    ppermute x0 -> x4, starting transfers between devices: none -> 18.5 us  [shards(): lax.ppermute(row_squares, 'outer', [(dev, dev ^ hop) for dev in range(16)])]
    another operation x8, local copies, waits for them, and re-layouts: 13.2 us -> 8.55 us  [shards(): jnp.stack([extended_values[place:place + groups_here] for place in range(...]
    slice x2 -> x1, local copies, waits for them, and re-layouts: 0.01 us -> 2.18 us  [shards(): running[:-1]]
  transfers between devices with their start and end apart: 4 -> 8, of which waited for: 1 -> 2; matrix products, arithmetic and copies ran while one was open for 26% -> 38% of each run, Pallas kernels for 0% -> 0%
where the time goes in v1:
time: 181 us; the launch traced here: 178 us
  waiting for transfers between devices  53.8 us (30%)
  other arithmetic  40 us (22%)
  starting transfers between devices  30.4 us (17%)
  local copies, waits for them, and re-layouts  29 us (16%)
  between operations  13.7 us (8%)
  matrix products  10.6 us (6%)
    all_gather x1, waiting for transfers between devices, carried_in(): gathered = lax.all_gather(part, axis)  52.6 us
    add x24, other arithmetic, add_states(): return earlier + later  22.5 us
    ppermute x4, starting transfers between devices, shards(): lax.ppermute(row_squares, 'outer', [(dev, dev ^ hop) for dev in range(16)])  18.5 us
    ppermute x3, starting transfers between devices, from_behind(): lax.ppermute(value, axis, [(source, source + steps) for source in range(f...  12 us
    another operation x8, local copies, waits for them, and re-layouts, shards(): jnp.stack([extended_values[place:place + groups_here] for place in range(...  8.55 us
    another operation x8, local copies, waits for them, and re-layouts, shards(): jnp.stack([extended_keys[place:place + groups_here] for place in range(PR...  7.26 us
    another operation x1, other arithmetic, shards(): jnp.stack([extended_values[place:place + groups_here] for place in range(...  6.26 us
    sub x1, other arithmetic, shards(): expd = jnp.exp(scores - largest)  3.86 us
  transfers between devices with their start and end apart: 8, of which 2 were waited for; matrix products, arithmetic and copies ran while one was open for 38% of the time, Pallas kernels for 0%

profile of v1, /device:TPU:7, one launch (start us, length us, event | category | flops | bytes accessed | tf_op | source)
XLA Modules:
  0.0 178.2 jit_solution(935824034905839882)
XLA Ops:
  7.3 1.2 broadcast_select_fusion
  8.7 1.2 reshape.85
  10.8 1.0 fusion.38
  11.9 1.6 slice.70
  14.2 4.0 %collective-permute-start.6 = (bf16[384,256]{1,0:T(8,128)(2,1)}, bf16[384,256]{1,0:T(8,128)(2,1)S(1)}, u32[]{:S(2)}, u32[]{:S(2)}) collective-permute-start(bf16[384,256]{1,0:T(8,128)(2,1)} %slice.79), channel_id=1, source_target_pairs={{0,1},{1,2},{2,3},{3,4},{4,5},{5,6},{6,7},{7,8},{8,9},{9,10},{10,1... | collective-permute-start | bytes 589832 | tf_op jit(solution)/shard_map/ppermute | solution.py:26
  18.3 4.0 %collective-permute-start.5 = (s32[3]{0:T(128)S(1)}, s32[3]{0:T(128)S(1)}, u32[]{:S(2)}, u32[]{:S(2)}) collective-permute-start(s32[3]{0:T(128)S(1)} %slice.61), channel_id=1, source_target_pairs={{0,1},{1,2},{2,3},{3,4},{4,5},{5,6},{6,7},{7,8},{8,9},{9,10},{10,1... | collective-permute-start | bytes 44 | tf_op jit(solution)/shard_map/ppermute | solution.py:26
  23.0 4.0 %collective-permute-start.4 = (bf16[384,256]{1,0:T(8,128)(2,1)}, bf16[384,256]{1,0:T(8,128)(2,1)}, u32[]{:S(2)}, u32[]{:S(2)}) collective-permute-start(bf16[384,256]{1,0:T(8,128)(2,1)} %slice.57), channel_id=1, source_target_pairs={{0,1},{1,2},{2,3},{3,4},{4,5},{5,6},{6,7},{7,8},{8,9},{9,10},{10,1... | collective-permute-start | bytes 589832 | tf_op jit(solution)/shard_map/ppermute | solution.py:26
  27.0 2.2 %slice.71 = f32[7,2,128,128]{3,2,1,0:T(8,128)} slice(f32[8,2,128,128]{3,2,1,0:T(8,128)} %fusion.38), slice={[0:7], [0:2], [0:128], [0:128]} | slice | bytes 1835008 | tf_op jit(solution)/shard_map/slice | solution.py:47
  30.2 1.2 reshape.86
  31.4 2.0 %copy.56 = bf16[8,1,128,2,128]{4,2,1,3,0:T(8,128)(2,1)} copy(bf16[8,1,128,2,128]{4,3,2,0,1:T(2,128)(2,1)} %stack.58) | data formatting | bytes 1048576 | tf_op jit(solution)/shard_map/stack | solution.py:69
  33.4 2.0 %copy.52 = bf16[8,1,128,2,128]{2,1,4,3,0:T(2,128)(2,1)} copy(bf16[8,1,128,2,128]{4,3,2,0,1:T(2,128)(2,1)S(1)} %stack.48) | data formatting | bytes 1048576 | tf_op jit(solution)/shard_map/stack | solution.py:72
  35.7 1.4 broadcast_and_fusion
  37.1 1.1 fusion.13
  38.2 1.2 stack.55
  40.3 1.2 stack.56
  42.6 1.6 pad_maximum_fusion.1
  45.3 3.9 %fusion.33 = (f32[8,2,128]{2,1,0:T(2,128)S(1)}, f32[8,2,128,512]{2,3,1,0:T(8,128)}) fusion(f32[8,2,512,128]{3,2,1,0:T(8,128)S(1)} %fusion.21, pred[8,128,512]{1,2,0:T(8,128)(4,1)S(1)} %copy-done.2), kind=kOutput, calls=%fused_computation.63 | output fusion | flops 6291967 | bytes 8921088 | tf_op jit(solution)/shard_map/sub | solution.py:93
  49.1 52.6 %all-gather.2.cloned.1.call-done = f32[32,2,128,128]{3,2,1,0:T(8,128)} async-done(((f32[1,2,128,128]{3,2,1,0:T(8,128)}), f32[32,2,128,128]{3,2,1,0:T(8,128)}) %all-gather.2.cloned.1.call-update) | async-done | bytes 4194320 | tf_op jit(solution)/shard_map/all_gather | solution.py:14
  101.7 23.1 %while.10 = (s32[]{:T(128)}, f32[2,128,128]{2,1,0:T(8,128)S(1)}, s32[]{:T(128)}, f32[32,2,128,128]{3,2,1,0:T(8,128)}, s32[]{:T(128)}, /*index=5*/s32[]{:T(128)}, s32[]{:T(128)}) while((s32[]{:T(128)}, f32[2,128,128]{2,1,0:T(8,128)S(1)}, s32[]{:T(128)}, f32[32,2,128,128]{3,2,1,0:T(8,128)}, s32[]{:T(128)}, /*index=5*/s32[]{:T(128)}, ...), condition=%wide.region_2.3_spmd, body=%wide.region_1.2_spmd.sunk | while | flops 32773 | bytes 393331 | solution.py:20
  124.9 2.7 %convolution_bitcast_fusion.2 = f32[8,128,2,128]{1,3,2,0:T(8,128)} fusion(f32[7,2,128,128]{3,2,1,0:T(8,128)} %slice.71, f32[2,128,128]{2,1,0:T(8,128)S(1)} %get-tuple-element.28, bf16[8,128,2,128]{3,2,1,0:T(2,128)(2,1)S(1)} %reshape.86), kind=kOutput, calls=%fused_computation.17 | convolution fusion | flops 67633152 | bytes 2621440 | tf_op jit(solution)/shard_map/cthd,chde->cthe/dot_general | solution.py:98
  127.6 2.9 %multiply_reduce_fusion = (f32[8,128]{1,0:T(8,128)S(1)}, f32[8,128,2,128]{1,3,2,0:T(8,128)}) fusion(f32[8,128,2,128]{1,3,2,0:T(8,128)} %convolution_bitcast_fusion.2, bf16[8,128,2,128]{1,3,2,0:T(8,128)(2,1)S(1)} %copy.48, pred[128,128]{0,1:T(8,128)(4,1)S(1)} %iota_compare_fusion, bf16[8,128,2,128]{3,2,1,0:T(2,128)(2,1)S(1)} %reshape.84, ...), kind=kOutput, calls=%fused_computation.21 | convolution fusion | flops 135527424 | bytes 3690496 | tf_op jit(solution)/shard_map/chts,cshe->cthe/dot_general | solution.py:105
  130.4 5.7 %collective-permute-start = (f32[8,128]{1,0:T(8,128)S(1)}, f32[8,128]{1,0:T(8,128)S(1)}, u32[]{:S(2)}, u32[]{:S(2)}) collective-permute-start(f32[8,128]{1,0:T(8,128)S(1)} %get-tuple-element.49), channel_id=1, source_target_pairs={{0,32},{32,0},{64,96},{96,64},{128,160},{160,128},{192,224},{224,1... | collective-permute-start | bytes 12296 | tf_op jit(solution)/shard_map/ppermute | solution.py:112
  137.1 3.1 %collective-permute-start.1 = (f32[8,128]{1,0:T(8,128)S(1)}, f32[8,128]{1,0:T(8,128)S(1)}, u32[]{:S(2)}, u32[]{:S(2)}) collective-permute-start(f32[8,128]{1,0:T(8,128)S(1)} %add.47), channel_id=1, source_target_pairs={{0,64},{32,96},{64,0},{96,32},{128,192},{160,224},{192,128},{224,1... | collective-permute-start | bytes 12296 | tf_op jit(solution)/shard_map/ppermute | solution.py:112
  140.3 1.2 collective-permute-done.1
  141.5 4.0 %collective-permute-start.2 = (f32[8,128]{1,0:T(8,128)S(1)}, f32[8,128]{1,0:T(8,128)S(1)}, u32[]{:S(2)}, u32[]{:S(2)}) collective-permute-start(f32[8,128]{1,0:T(8,128)S(1)} %add.48), channel_id=1, source_target_pairs={{0,128},{32,160},{64,192},{96,224},{128,0},{160,32},{192,64},{224,... | collective-permute-start | bytes 12296 | tf_op jit(solution)/shard_map/ppermute | solution.py:112
  145.8 2.0 %copy.49 = bf16[8,1,128,2,128]{2,1,4,3,0:T(2,128)(2,1)} copy(bf16[8,1,128,2,128]{4,3,2,0,1:T(2,128)(2,1)S(1)} %stack.45) | data formatting | bytes 1048576 | tf_op jit(solution)/shard_map/stack | solution.py:72
  147.9 2.0 %copy.50 = bf16[8,1,128,2,128]{2,1,4,3,0:T(2,128)(2,1)} copy(bf16[8,1,128,2,128]{4,3,2,0,1:T(2,128)(2,1)S(1)} %stack.46) | data formatting | bytes 1048576 | tf_op jit(solution)/shard_map/stack | solution.py:72
  150.1 2.0 %copy.51 = bf16[8,1,128,2,128]{2,1,4,3,0:T(2,128)(2,1)} copy(bf16[8,1,128,2,128]{4,3,2,0,1:T(2,128)(2,1)S(1)} %stack.47) | data formatting | bytes 1048576 | tf_op jit(solution)/shard_map/stack | solution.py:72
  152.1 5.6 %collective-permute-start.3 = (f32[8,128]{1,0:T(8,128)S(1)}, f32[8,128]{1,0:T(8,128)S(1)}, u32[]{:S(2)}, u32[]{:S(2)}) collective-permute-start(f32[8,128]{1,0:T(8,128)S(1)} %add.49), channel_id=1, source_target_pairs={{0,256},{32,288},{64,320},{96,352},{128,384},{160,416},{192,448},{... | collective-permute-start | bytes 12296 | tf_op jit(solution)/shard_map/ppermute | solution.py:112
  157.7 6.3 %pad_maximum_fusion = bf16[8,4,128,2,128]{2,1,4,3,0:T(4,128)(2,1)S(1)} fusion(bf16[8,1,128,2,128]{2,1,4,3,0:T(2,128)(2,1)S(1)} %copy-done.1, bf16[8,1,128,2,128]{2,1,4,3,0:T(2,128)(2,1)} %copy.51, bf16[8,1,128,2,128]{2,1,4,3,0:T(2,128)(2,1)} %copy.50, bf16[8,1,128,2,128]{2,1,4,3,0:T(2,128)(2,1)} %copy.49), kind=kLoop, calls=%fused_computation.6 | loop fusion | flops 8388608 | bytes 4194304 | tf_op jit(solution)/shard_map/stack | solution.py:72
  163.9 2.2 %reshape.87 = bf16[8,512,2,128]{1,3,2,0:T(8,128)(2,1)} reshape(bf16[8,4,128,2,128]{2,1,4,3,0:T(4,128)(2,1)S(1)} %pad_maximum_fusion) | data formatting | bytes 4194304 | tf_op jit(solution)/shard_map/reshape | solution.py:74
  166.2 3.8 %fusion.10 = bf16[8,128,2,128]{1,3,2,0:T(8,128)(2,1)S(1)} fusion(bf16[8,512,2,128]{1,3,2,0:T(8,128)(2,1)} %reshape.87, f32[8,2,128,512]{2,3,1,0:T(8,128)} %get-tuple-element.48, f32[8,2,128]{2,1,0:T(2,128)S(1)} %get-tuple-element.47, f32[8,128,2,128]{1,3,2,0:T(8,128)} %get-tuple-element.50, f32[2,128]{1,0:T(2,128)S(1)} %bitcast.65, ...), kind=kOutput, calls=%fused_computation.19 | convolution fusion | flops 271581184 | bytes 7877632 | tf_op jit(solution)/shard_map/chts,cshd->cthd/dot_general | solution.py:95
  (80 shorter events, 33.1 us)
Async XLA Ops:
  6.5 95.2 %all-gather.2.cloned.1.call-start = ((), (), s32[]{:S(2)}) async-start(), calls=%async_computation | async-start | bytes 4325376 | tf_op jit(solution)/shard_map/all_gather | solution.py:14
  8.5 9.7 %copy-start.5 = (s32[8]{0:T(128)S(1)}, s32[8]{0:T(128)}, u32[]{:S(2)}) copy-start(s32[8]{0:T(128)} %param.11) | copy-start | bytes 100
  8.5 13.7 %copy-start = (bf16[1024,256]{1,0:T(8,128)(2,1)S(1)}, bf16[1024,256]{1,0:T(8,128)(2,1)}, u32[]{:S(2)}) copy-start(bf16[1024,256]{1,0:T(8,128)(2,1)} %param.10) | copy-start | bytes 1572868
  10.8 22.5 %copy-start.3 = (s32[8,3]{0,1:T(4,128)S(1)}, s32[8,3]{0,1:T(4,128)}, u32[]{:S(2)}) copy-start(s32[8,3]{0,1:T(4,128)} %param.12) | copy-start | bytes 292
  14.2 22.9 %collective-permute-start.6 = (bf16[384,256]{1,0:T(8,128)(2,1)}, bf16[384,256]{1,0:T(8,128)(2,1)S(1)}, u32[]{:S(2)}, u32[]{:S(2)}) collective-permute-start(bf16[384,256]{1,0:T(8,128)(2,1)} %slice.79), channel_id=1, source_target_pairs={{0,1},{1,2},{2,3},{3,4},{4,5},{5,6},{6,7},{7,8},{8,9},{9,10},{10,1... | collective-permute-start | bytes 589832 | tf_op jit(solution)/shard_map/ppermute | solution.py:26
  18.3 17.2 %collective-permute-start.5 = (s32[3]{0:T(128)S(1)}, s32[3]{0:T(128)S(1)}, u32[]{:S(2)}, u32[]{:S(2)}) collective-permute-start(s32[3]{0:T(128)S(1)} %slice.61), channel_id=1, source_target_pairs={{0,1},{1,2},{2,3},{3,4},{4,5},{5,6},{6,7},{7,8},{8,9},{9,10},{10,1... | collective-permute-start | bytes 44 | tf_op jit(solution)/shard_map/ppermute | solution.py:26
  23.0 113.2 %collective-permute-start.4 = (bf16[384,256]{1,0:T(8,128)(2,1)}, bf16[384,256]{1,0:T(8,128)(2,1)}, u32[]{:S(2)}, u32[]{:S(2)}) collective-permute-start(bf16[384,256]{1,0:T(8,128)(2,1)} %slice.57), channel_id=1, source_target_pairs={{0,1},{1,2},{2,3},{3,4},{4,5},{5,6},{6,7},{7,8},{8,9},{9,10},{10,1... | collective-permute-start | bytes 589832 | tf_op jit(solution)/shard_map/ppermute | solution.py:26
  44.2 1.1 copy-start.2
  130.4 6.7 %collective-permute-start = (f32[8,128]{1,0:T(8,128)S(1)}, f32[8,128]{1,0:T(8,128)S(1)}, u32[]{:S(2)}, u32[]{:S(2)}) collective-permute-start(f32[8,128]{1,0:T(8,128)S(1)} %get-tuple-element.49), channel_id=1, source_target_pairs={{0,32},{32,0},{64,96},{96,64},{128,160},{160,128},{192,224},{224,1... | collective-permute-start | bytes 12296 | tf_op jit(solution)/shard_map/ppermute | solution.py:112
  137.1 4.4 %collective-permute-start.1 = (f32[8,128]{1,0:T(8,128)S(1)}, f32[8,128]{1,0:T(8,128)S(1)}, u32[]{:S(2)}, u32[]{:S(2)}) collective-permute-start(f32[8,128]{1,0:T(8,128)S(1)} %add.47), channel_id=1, source_target_pairs={{0,64},{32,96},{64,0},{96,32},{128,192},{160,224},{192,128},{224,1... | collective-permute-start | bytes 12296 | tf_op jit(solution)/shard_map/ppermute | solution.py:112
  141.5 10.6 %collective-permute-start.2 = (f32[8,128]{1,0:T(8,128)S(1)}, f32[8,128]{1,0:T(8,128)S(1)}, u32[]{:S(2)}, u32[]{:S(2)}) collective-permute-start(f32[8,128]{1,0:T(8,128)S(1)} %add.48), channel_id=1, source_target_pairs={{0,128},{32,160},{64,192},{96,224},{128,0},{160,32},{192,64},{224,... | collective-permute-start | bytes 12296 | tf_op jit(solution)/shard_map/ppermute | solution.py:112
  145.6 12.0 %copy-start.1 = (bf16[8,1,128,2,128]{2,1,4,3,0:T(2,128)(2,1)S(1)}, bf16[8,1,128,2,128]{2,1,4,3,0:T(2,128)(2,1)}, u32[]{:S(2)}) copy-start(bf16[8,1,128,2,128]{2,1,4,3,0:T(2,128)(2,1)} %copy.52) | copy-start | bytes 1572868
  152.1 14.1 %copy-start.4 = (f32[256]{0:T(256)S(1)}, f32[256]{0:T(256)}, u32[]{:S(2)}) copy-start(f32[256]{0:T(256)} %param.13) | copy-start | bytes 3076
  152.1 14.1 %collective-permute-start.3 = (f32[8,128]{1,0:T(8,128)S(1)}, f32[8,128]{1,0:T(8,128)S(1)}, u32[]{:S(2)}, u32[]{:S(2)}) collective-permute-start(f32[8,128]{1,0:T(8,128)S(1)} %add.49), channel_id=1, source_target_pairs={{0,256},{32,288},{64,320},{96,352},{128,384},{160,416},{192,448},{... | collective-permute-start | bytes 12296 | tf_op jit(solution)/shard_map/ppermute | solution.py:112
Sparse Core Ops, SparseCore 0:
  13.6 88.0 all-gather.1
